TPU v7x, 32 devices: a whole 2x2x4 slice. The times are simulated.
32 devices in a mesh: layer: 4 (over y, core), latent: 8 (over z, x).
Axes of the slice: x: 2, y: 2, z: 4, core: 2. Of those that a mesh axis runs over, the one named last changes fastest.
Arguments:
- inputs: bfloat16 [4, 128, 4096], P('layer', 'latent'), may hold values from -6 to 6
- targets: bfloat16 [4, 128, 4096], P('layer', 'latent'), may hold values from -6 to 6
- w_enc: bfloat16 [4, 4096, 8192], P('layer', None, 'latent'), may hold values from -0.09375 to 0.09375
- b_enc: float32 [4, 8192], P('layer', 'latent'), may hold values from -3 to 3
- w_dec: bfloat16 [4, 4, 8192, 4096], P('layer', None, 'latent'), may hold values from -0.03125 to 0.03125
- b_dec: float32 [4, 4096], P('layer'), may hold values from -3 to 3
Outputs:
- grad_enc: bfloat16 [4, 4096, 8192], P('layer', None, 'latent')
- grad_benc: float32 [4, 8192], P('layer', 'latent')
- grad_dec: bfloat16 [4, 4, 8192, 4096], P('layer', None, 'latent')
- grad_bdec: float32 [4, 4096], P('layer')
All inputs are finite; a program needn't handle non-finite values.
Results may differ from a plain program's by a relative error of at most 0.0057.
Values may be sent and summed in bfloat16 or wider, within the bound.
A program may use at most 192 MiB of HBM per device.

v0:
```python
import jax
import jax.numpy as jnp
from jax import lax
from jax.sharding import PartitionSpec as P

penalty = 0.5
eps = 1e-06


def local(inputs, targets, w_enc, b_enc, w_dec, b_dec):
    source = lax.axis_index("layer")
    depth = w_dec.shape[1]
    whole = lax.all_gather(inputs[0], "latent", axis=0, tiled=True)
    pre = jnp.dot(whole, w_enc[0], preferred_element_type=jnp.float32) + b_enc[0]
    positive = jnp.maximum(pre, 0.0)
    act = (positive * positive).astype(jnp.bfloat16)
    valid = (jnp.arange(depth, dtype=jnp.int32) >= source).astype(jnp.float32)
    partial_value = (
        jnp.einsum("nk,tkd->tnd", act, w_dec[0], preferred_element_type=jnp.float32)
        * valid[:, None, None]
    )
    spread = lax.psum_scatter(partial_value, "layer", scatter_dimension=0, tiled=True)
    recon = lax.psum_scatter(spread, "latent", scatter_dimension=1, tiled=True)
    error = recon[0] + b_dec[0] - targets[0].astype(jnp.float32)
    grad_bdec = lax.psum(jnp.sum(error, axis=0), "latent")[None, :]
    err_low = error.astype(jnp.bfloat16)[None]
    stacked = lax.all_gather(err_low, "latent", axis=1, tiled=True)
    errors = lax.all_gather(stacked, "layer", axis=0, tiled=True)
    errors = jnp.where(valid[:, None, None] > 0.0, errors, jnp.zeros_like(errors))
    decoders = w_dec[0]
    squares = jnp.sum(jnp.square(decoders.astype(jnp.float32)), axis=2)
    norms = jnp.sqrt(jnp.sum(squares * valid[:, None], axis=0) + eps)
    back = jnp.einsum("tnd,tkd->nk", errors, decoders, preferred_element_type=jnp.float32)
    d_act = back + penalty * norms[None, :]
    d_pre = d_act * 2.0 * positive
    grad_benc = jnp.sum(d_pre, axis=0)[None, :]
    d_low = d_pre.astype(jnp.bfloat16)
    grad_enc = lax.dot_general(
        whole, d_low, (((0,), (0,)), ((), ())), preferred_element_type=jnp.float32
    ).astype(jnp.bfloat16)[None]
    act_total = jnp.sum(act.astype(jnp.float32), axis=0)
    scale = penalty * act_total / norms
    grad_mse = jnp.einsum("nk,tnd->tkd", act, errors, preferred_element_type=jnp.float32)
    shrink = valid[:, None, None] * scale[None, :, None] * decoders.astype(jnp.float32)
    grad_dec = (grad_mse + shrink).astype(jnp.bfloat16)[None]
    return (grad_enc, grad_benc, grad_dec, grad_bdec)


def solution(mesh):
    placed = (
        P("layer", "latent", None),
        P("layer", "latent", None),
        P("layer", None, "latent"),
        P("layer", "latent"),
        P("layer", None, "latent", None),
        P("layer", None),
    )
    return jax.shard_map(
        local,
        mesh=mesh,
        in_specs=placed,
        out_specs=(
            P("layer", None, "latent"),
            P("layer", "latent"),
            P("layer", None, "latent", None),
            P("layer", None),
        ),
        check_vma=False,
    )
```

profile of v0, /device:TPU:0, one launch (start us, length us, event | category | flops | bytes accessed | tf_op | source)
XLA Modules:
  0.0 456.9 jit_solution(2697420618974324879)
XLA Ops:
  7.2 0.0 all-gather.9.cloned.1.call-start
  7.2 0.7 all-gather.9.cloned.1.call-update
  7.9 0.0 reduce-scatter.3.cloned.1.call-start
  8.0 45.2 %all-gather.9.cloned.1.call-done = bf16[1,128,4096]{2,1,0:T(8,128)(2,1)} async-done(((bf16[1,16,4096]{2,1,0:T(8,128)(2,1)}), bf16[1,128,4096]{2,1,0:T(8,128)(2,1)}) %all-gather.9.cloned.1.call-update) | async-done | bytes 1048592 | tf_op jit(solution)/shard_map/all_gather | solution.py:13
  53.1 4.9 %convert_reduce_fusion = (f32[1024]{0:T(1024)S(1)}, f32[128,1024]{1,0:T(8,128)S(1)}) fusion(f32[1024]{0:T(1024)} %bitcast.82, bf16[1,4096,1024]{2,1,0:T(8,128)(2,1)} %param.8, bf16[1,128,4096]{2,1,0:T(8,128)(2,1)} %all-gather.9.cloned.1.call-done), kind=kOutput, calls=%fused_computation.23 | convolution fusion | flops 1074527232 | bytes 9969664 | tf_op jit(solution)/shard_map/dot_general | solution.py:14
  58.0 18.5 %multiply_bitcast_fusion = f32[4,128,4096]{2,1,0:T(8,128)} fusion(f32[4]{0:T(128)S(1)} %compare_convert_fusion, bf16[1,4,1024,4096]{3,2,1,0:T(8,128)(2,1)} %param.10, f32[128,1024]{1,0:T(8,128)S(1)} %get-tuple-element.15), kind=kOutput, calls=%fused_computation.13 | convolution fusion | flops 4297326592 | bytes 42467344 | tf_op jit(solution)/shard_map/nk,tkd->tnd/dot_general | solution.py:19
  76.5 0.0 copy-start.2
  76.5 0.0 copy-start.3
  76.5 0.0 reduce-scatter.3.cloned.1.call-update
  76.6 0.0 reduce-scatter.5.cloned.1.call-start
  76.6 70.2 %reduce-scatter.3.cloned.1.call-done = f32[1,128,4096]{2,1,0:T(8,128)} async-done(((f32[4,128,4096]{2,1,0:T(8,128)}), f32[1,128,4096]{2,1,0:T(8,128)}) %reduce-scatter.3.cloned.1.call-update) | async-done | bytes 2097168 | tf_op jit(solution)/shard_map/reduce_scatter | solution.py:22
  146.9 0.0 reduce-scatter.5.cloned.1.call-update
  146.9 0.0 all-gather.5.cloned.1.call-start
  146.9 72.2 %reduce-scatter.5.cloned.1.call-done = f32[1,16,4096]{2,1,0:T(8,128)} async-done(((f32[1,128,4096]{2,1,0:T(8,128)}), f32[1,16,4096]{2,1,0:T(8,128)}) %reduce-scatter.5.cloned.1.call-update) | async-done | bytes 262160 | tf_op jit(solution)/shard_map/reduce_scatter | solution.py:23
  219.2 0.0 copy-done.2
  219.2 0.0 copy-done.3
  219.2 1.6 fusion.32
  220.8 0.0 all-gather.5.cloned.1.call-update
  220.8 0.0 all-gather.7.cloned.1.call-start
  220.9 40.2 %all-gather.5.cloned.1.call-done = bf16[1,128,4096]{2,1,0:T(8,128)(2,1)} async-done(((bf16[1,16,4096]{2,1,0:T(8,128)(2,1)}), bf16[1,128,4096]{2,1,0:T(8,128)(2,1)}) %all-gather.5.cloned.1.call-update) | async-done | bytes 1048592 | tf_op jit(solution)/shard_map/all_gather | solution.py:27
  261.1 0.0 all-gather.7.cloned.1.call-update
  261.1 40.6 %copy.16 = bf16[1,4,1024,4096]{2,3,1,0:T(8,128)(2,1)} copy(bf16[1,4,1024,4096]{3,2,1,0:T(8,128)(2,1)} %param.10) | data formatting | bytes 67108864 | tf_op args[4]
  301.6 0.0 copy-start.1
  301.7 11.7 %fusion = f32[4,1024]{1,0:T(4,128)S(1)} fusion(bf16[1,4,1024,4096]{2,3,1,0:T(8,128)(2,1)} %copy.16), kind=kLoop, calls=%fused_computation.2 | loop fusion | flops 50327552 | bytes 33570816 | tf_op jit(solution)/shard_map/reduce_sum | solution.py:31
  313.4 0.1 multiply_reduce_fusion
  313.5 0.1 broadcast_multiply_fusion
  313.5 0.0 copy-done.1
  313.5 0.1 fusion.34
  313.6 35.7 %psum.7 = f32[1,4096]{1,0:T(1,128)} all-reduce(f32[1,4096]{1,0:T(1,128)S(1)} %bitcast.81), channel_id=1, replica_groups=mesh['layer'=4,'latent'=8] {'latent'}, use_global_device_ids=true, to_apply=%region_7.8 | all-reduce | flops 4096 | bytes 32768 | tf_op jit(solution)/shard_map/psum | solution.py:25
  349.3 0.0 all-gather.7.cloned.1.call-done
  349.3 25.4 %fusion.7 = bf16[1,4,1024,4096]{2,3,1,0:T(8,128)(2,1)} fusion(bf16[1,4,1024,4096]{2,3,1,0:T(8,128)(2,1)} %copy.16, f32[4,1024]{1,0:T(4,128)S(1)} %broadcast_multiply_fusion, bf16[4,128,4096]{2,1,0:T(8,128)(2,1)} %all-gather.7.cloned.1.call-done, pred[4]{0:T(512)(128)(4,1)S(1)} %broadcast_compare_fusion, f32[128,1024]{1,0:T(8,128)S(1)} %get-tuple-element.15), kind=kOutput, calls=%fused_computation.9 | convolution fusion | flops 4364435456 | bytes 71843840 | tf_op jit(solution)/shard_map/nk,tnd->tkd/dot_general | solution.py:43
  374.7 40.5 %copy.21 = bf16[1,4,1024,4096]{3,2,1,0:T(8,128)(2,1)} copy(bf16[1,4,1024,4096]{2,3,1,0:T(8,128)(2,1)} %fusion.7) | data formatting | bytes 67108864
  415.2 0.0 copy-start
  415.2 17.6 %fusion.40 = (f32[1024]{0:T(1024)}, bf16[128,1024]{1,0:T(8,128)(2,1)S(1)}) fusion(f32[128,1024]{1,0:T(8,128)S(1)} %get-tuple-element.15, f32[1024]{0:T(1024)S(1)} %get-tuple-element.13, bf16[1,4,1024,4096]{3,2,1,0:T(8,128)(2,1)} %param.10, bf16[4,128,4096]{2,1,0:T(8,128)(2,1)} %all-gather.7.cloned.1.call-done, pred[4]{0:T(512)(128)(4,1)S(1)} %broadcast_compare_fusion), kind=kOutput, calls=%fused_computation.42 | convolution fusion | flops 4297718784 | bytes 38543364 | tf_op jit(solution)/shard_map/tnd,tkd->nk/dot_general | solution.py:33
  432.8 0.0 copy-done
  432.8 5.6 %convert_bitcast_fusion = bf16[1,4096,1024]{1,2,0:T(8,128)(2,1)} fusion(bf16[1,128,4096]{2,1,0:T(8,128)(2,1)S(1)} %copy-done, bf16[128,1024]{1,0:T(8,128)(2,1)S(1)} %get-tuple-element.17), kind=kOutput, calls=%fused_computation.12 | convolution fusion | flops 1077936128 | bytes 9699328 | tf_op jit(solution)/shard_map/dot_general | solution.py:38
  438.4 11.9 %copy.20 = bf16[1,4096,1024]{2,1,0:T(8,128)(2,1)} copy(bf16[1,4096,1024]{1,2,0:T(8,128)(2,1)} %convert_bitcast_fusion) | data formatting | bytes 16777216
  (3 shorter events, 0.0 us)
Async XLA Ops:
  7.2 46.0 %all-gather.9.cloned.1.call-start = ((), (), s32[]{:S(2)}) async-start(), calls=%async_computation.6 | async-start | bytes 1179648 | tf_op jit(solution)/shard_map/all_gather | solution.py:13
  7.9 139.0 %reduce-scatter.3.cloned.1.call-start = ((), (), s32[]{:S(2)}) async-start(), calls=%async_computation.2 | async-start | bytes 10485760 | tf_op jit(solution)/shard_map/reduce_scatter | solution.py:22
  76.5 142.6 %copy-start.2 = (bf16[1,16,4096]{2,1,0:T(8,128)(2,1)S(1)}, bf16[1,16,4096]{2,1,0:T(8,128)(2,1)}, u32[]{:S(2)}) copy-start(bf16[1,16,4096]{2,1,0:T(8,128)(2,1)} %param.7) | copy-start | bytes 393220
  76.5 142.6 %copy-start.3 = (f32[1,4096]{1,0:T(1,128)S(1)}, f32[1,4096]{1,0:T(1,128)}, u32[]{:S(2)}) copy-start(f32[1,4096]{1,0:T(1,128)} %param.11) | copy-start | bytes 49156
  76.6 142.6 %reduce-scatter.5.cloned.1.call-start = ((), (), s32[]{:S(2)}) async-start(), calls=%async_computation.3 | async-start | bytes 2359296 | tf_op jit(solution)/shard_map/reduce_scatter | solution.py:23
  146.9 114.2 %all-gather.5.cloned.1.call-start = ((), (), s32[]{:S(2)}) async-start(), calls=%async_computation.4 | async-start | bytes 1179648 | tf_op jit(solution)/shard_map/all_gather | solution.py:27
  220.8 128.5 %all-gather.7.cloned.1.call-start = ((), (), s32[]{:S(2)}) async-start(), calls=%async_computation.5 | async-start | bytes 5242880 | tf_op jit(solution)/shard_map/all_gather | solution.py:28
  301.6 11.9 %copy-start.1 = (f32[1,16,4096]{2,1,0:T(8,128)S(1)}, f32[1,16,4096]{2,1,0:T(8,128)}, u32[]{:S(2)}) copy-start(f32[1,16,4096]{2,1,0:T(8,128)} %reduce-scatter.5.cloned.1.call-done) | copy-start | bytes 786436
  415.2 17.6 %copy-start = (bf16[1,128,4096]{2,1,0:T(8,128)(2,1)S(1)}, bf16[1,128,4096]{2,1,0:T(8,128)(2,1)}, u32[]{:S(2)}) copy-start(bf16[1,128,4096]{2,1,0:T(8,128)(2,1)} %all-gather.9.cloned.1.call-done) | copy-start | bytes 3145732
Sparse Core Ops, SparseCore 0:
  10.1 42.9 all-gather.8
  76.7 70.1 reduce-scatter.2
  150.4 68.7 reduce-scatter.4
  221.7 39.2 all-gather.4
  262.5 33.1 all-gather.6
where the time goes:
time: 459 us; the launch traced here: 457 us
  waiting for transfers between devices  229 us (50%)
  local copies, waits for them, and re-layouts  93 us (20%)
  matrix products  72 us (16%)
  blocking collectives  35.7 us (8%)
  between operations  13.8 us (3%)
  other arithmetic  13.6 us (3%)
    unnamed x11, local copies, waits for them, and re-layouts  93 us
    reduce_scatter x1, waiting for transfers between devices, local(): recon = lax.psum_scatter(spread, 'latent', scatter_dimension=1, tiled=True)  72.2 us
    reduce_scatter x1, waiting for transfers between devices, local(): lax.psum_scatter(partial_value, 'layer', scatter_dimension=0, tiled=True)  70.2 us
    all_gather x1, waiting for transfers between devices, local(): whole = lax.all_gather(inputs[0], 'latent', axis=0, tiled=True)  45.2 us
    all_gather x1, waiting for transfers between devices, local(): stacked = lax.all_gather(err_low, 'latent', axis=1, tiled=True)  40.2 us
    psum x1, blocking collectives, local(): grad_bdec = lax.psum(jnp.sum(error, axis=0), 'latent')[None, :]  35.7 us
    dot_general x1, matrix products, local(): jnp.einsum('nk,tnd->tkd', act, errors, preferred_element_type=jnp.float32)  25.4 us
    dot_general x1, matrix products, local(): jnp.einsum('nk,tkd->tnd', act, w_dec[0], preferred_element_type=jnp.float32)  18.5 us
  transfers between devices with their start and end apart: 5, of which 4 were waited for; matrix products, arithmetic and copies ran while one was open for 11% of the time, Pallas kernels for 0%

commit v1 on v0

--- a/solution.py
+++ b/solution.py
@@ -22,7 +22,7 @@
     spread = lax.psum_scatter(partial_value, "layer", scatter_dimension=0, tiled=True)
     recon = lax.psum_scatter(spread, "latent", scatter_dimension=1, tiled=True)
     error = recon[0] + b_dec[0] - targets[0].astype(jnp.float32)
-    grad_bdec = lax.psum(jnp.sum(error, axis=0), "latent")[None, :]
+    grad_bdec = jnp.sum(lax.all_gather(jnp.sum(error, axis=0), "latent"), axis=0)[None, :]
     err_low = error.astype(jnp.bfloat16)[None]
     stacked = lax.all_gather(err_low, "latent", axis=1, tiled=True)
     errors = lax.all_gather(stacked, "layer", axis=0, tiled=True)

time: 459 us -> 455 us (level)
  blocking collectives: 35.7 us -> 30.9 us
    psum x1 -> x0, blocking collectives: 35.7 us -> none  [local(): grad_bdec = lax.psum(jnp.sum(error, axis=0), 'latent')[None, :]]
    all_gather x0 -> x1, blocking collectives: none -> 30.9 us  [local(): lax.all_gather(jnp.sum(error, axis=0), 'latent')]
  transfers between devices with their start and end apart: 5 -> 5, of which waited for: 4 -> 4; matrix products, arithmetic and copies ran while one was open for 11% -> 12% of each run, Pallas kernels for 0% -> 0%
where the time goes in v1:
time: 455 us; the launch traced here: 453 us
  waiting for transfers between devices  229 us (50%)
  local copies, waits for them, and re-layouts  93 us (20%)
  matrix products  72.1 us (16%)
  blocking collectives  30.9 us (7%)
  other arithmetic  14.2 us (3%)
  between operations  13.8 us (3%)
    unnamed x11, local copies, waits for them, and re-layouts  93 us
    reduce_scatter x1, waiting for transfers between devices, local(): recon = lax.psum_scatter(spread, 'latent', scatter_dimension=1, tiled=True)  72.2 us
    reduce_scatter x1, waiting for transfers between devices, local(): lax.psum_scatter(partial_value, 'layer', scatter_dimension=0, tiled=True)  70.2 us
    all_gather x1, waiting for transfers between devices, local(): whole = lax.all_gather(inputs[0], 'latent', axis=0, tiled=True)  45.2 us
    all_gather x1, waiting for transfers between devices, local(): stacked = lax.all_gather(err_low, 'latent', axis=1, tiled=True)  40.2 us
    all_gather x1, blocking collectives, local(): lax.all_gather(jnp.sum(error, axis=0), 'latent')  30.9 us
    dot_general x1, matrix products, local(): jnp.einsum('nk,tnd->tkd', act, errors, preferred_element_type=jnp.float32)  25.5 us
    dot_general x1, matrix products, local(): jnp.einsum('nk,tkd->tnd', act, w_dec[0], preferred_element_type=jnp.float32)  18.5 us
  transfers between devices with their start and end apart: 5, of which 4 were waited for; matrix products, arithmetic and copies ran while one was open for 12% of the time, Pallas kernels for 0%

profile of v1, /device:TPU:0, one launch (start us, length us, event | category | flops | bytes accessed | tf_op | source)
XLA Modules:
  0.0 452.7 jit_solution(14499993240791043585)
XLA Ops:
  7.2 0.0 all-gather.10.cloned.1.call-start
  7.2 0.7 all-gather.10.cloned.1.call-update
  7.9 0.0 reduce-scatter.3.cloned.1.call-start
  8.0 45.2 %all-gather.10.cloned.1.call-done = bf16[1,128,4096]{2,1,0:T(8,128)(2,1)} async-done(((bf16[1,16,4096]{2,1,0:T(8,128)(2,1)}), bf16[1,128,4096]{2,1,0:T(8,128)(2,1)}) %all-gather.10.cloned.1.call-update) | async-done | bytes 1048592 | tf_op jit(solution)/shard_map/all_gather | solution.py:13
  53.1 4.9 %convert_reduce_fusion = (f32[1024]{0:T(1024)S(1)}, f32[128,1024]{1,0:T(8,128)S(1)}) fusion(f32[1024]{0:T(1024)} %bitcast.82, bf16[1,4096,1024]{2,1,0:T(8,128)(2,1)} %param.8, bf16[1,128,4096]{2,1,0:T(8,128)(2,1)} %all-gather.10.cloned.1.call-done), kind=kOutput, calls=%fused_computation.23 | convolution fusion | flops 1074527232 | bytes 9969664 | tf_op jit(solution)/shard_map/dot_general | solution.py:14
  58.0 18.5 %multiply_bitcast_fusion = f32[4,128,4096]{2,1,0:T(8,128)} fusion(f32[4]{0:T(128)S(1)} %compare_convert_fusion, bf16[1,4,1024,4096]{3,2,1,0:T(8,128)(2,1)} %param.10, f32[128,1024]{1,0:T(8,128)S(1)} %get-tuple-element.19), kind=kOutput, calls=%fused_computation.13 | convolution fusion | flops 4297326592 | bytes 42467344 | tf_op jit(solution)/shard_map/nk,tkd->tnd/dot_general | solution.py:19
  76.5 0.0 copy-start.2
  76.5 0.0 copy-start.3
  76.5 0.0 reduce-scatter.3.cloned.1.call-update
  76.6 0.0 reduce-scatter.5.cloned.1.call-start
  76.6 70.2 %reduce-scatter.3.cloned.1.call-done = f32[1,128,4096]{2,1,0:T(8,128)} async-done(((f32[4,128,4096]{2,1,0:T(8,128)}), f32[1,128,4096]{2,1,0:T(8,128)}) %reduce-scatter.3.cloned.1.call-update) | async-done | bytes 2097168 | tf_op jit(solution)/shard_map/reduce_scatter | solution.py:22
  146.9 0.0 reduce-scatter.5.cloned.1.call-update
  146.9 0.0 all-gather.6.cloned.1.call-start
  146.9 72.2 %reduce-scatter.5.cloned.1.call-done = f32[1,16,4096]{2,1,0:T(8,128)} async-done(((f32[1,128,4096]{2,1,0:T(8,128)}), f32[1,16,4096]{2,1,0:T(8,128)}) %reduce-scatter.5.cloned.1.call-update) | async-done | bytes 262160 | tf_op jit(solution)/shard_map/reduce_scatter | solution.py:23
  219.2 0.0 copy-done.2
  219.2 0.0 copy-done.3
  219.2 1.6 fusion.32
  220.8 0.0 all-gather.6.cloned.1.call-update
  220.8 0.0 all-gather.8.cloned.1.call-start
  220.9 40.2 %all-gather.6.cloned.1.call-done = bf16[1,128,4096]{2,1,0:T(8,128)(2,1)} async-done(((bf16[1,16,4096]{2,1,0:T(8,128)(2,1)}), bf16[1,128,4096]{2,1,0:T(8,128)(2,1)}) %all-gather.6.cloned.1.call-update) | async-done | bytes 1048592 | tf_op jit(solution)/shard_map/all_gather | solution.py:27
  261.1 0.0 all-gather.8.cloned.1.call-update
  261.1 40.6 %copy.22 = bf16[1,4,1024,4096]{2,3,1,0:T(8,128)(2,1)} copy(bf16[1,4,1024,4096]{3,2,1,0:T(8,128)(2,1)} %param.10) | data formatting | bytes 67108864 | tf_op args[4]
  301.6 0.0 copy-start.1
  301.7 11.7 %fusion = f32[4,1024]{1,0:T(4,128)S(1)} fusion(bf16[1,4,1024,4096]{2,3,1,0:T(8,128)(2,1)} %copy.22), kind=kLoop, calls=%fused_computation.2 | loop fusion | flops 50327552 | bytes 33570816 | tf_op jit(solution)/shard_map/reduce_sum | solution.py:31
  313.4 0.1 multiply_reduce_fusion
  313.5 0.1 broadcast_multiply_fusion
  313.5 0.0 copy-done.1
  313.5 0.1 fusion.34
  313.6 30.9 %all-gather.1 = f32[32768]{0:T(1024)S(1)} all-gather(f32[4096]{0:T(1024)S(1)} %fusion.34), channel_id=3, replica_groups=mesh['layer'=4,'latent'=8] {'latent'}, dimensions={0}, use_global_device_ids=true | all-gather | bytes 147456 | tf_op jit(solution)/shard_map/all_gather | solution.py:25
  344.5 0.6 reduce_sum.59
  345.2 0.0 all-gather.8.cloned.1.call-done
  345.2 25.5 %fusion.7 = bf16[1,4,1024,4096]{2,3,1,0:T(8,128)(2,1)} fusion(bf16[1,4,1024,4096]{2,3,1,0:T(8,128)(2,1)} %copy.22, f32[4,1024]{1,0:T(4,128)S(1)} %broadcast_multiply_fusion, bf16[4,128,4096]{2,1,0:T(8,128)(2,1)} %all-gather.8.cloned.1.call-done, pred[4]{0:T(512)(128)(4,1)S(1)} %broadcast_compare_fusion, f32[128,1024]{1,0:T(8,128)S(1)} %get-tuple-element.19), kind=kOutput, calls=%fused_computation.9 | convolution fusion | flops 4364435456 | bytes 71843840 | tf_op jit(solution)/shard_map/nk,tnd->tkd/dot_general | solution.py:43
  370.6 40.5 %copy.27 = bf16[1,4,1024,4096]{3,2,1,0:T(8,128)(2,1)} copy(bf16[1,4,1024,4096]{2,3,1,0:T(8,128)(2,1)} %fusion.7) | data formatting | bytes 67108864
  411.1 0.0 copy-start
  411.1 17.6 %fusion.40 = (f32[1024]{0:T(1024)}, bf16[128,1024]{1,0:T(8,128)(2,1)S(1)}) fusion(f32[128,1024]{1,0:T(8,128)S(1)} %get-tuple-element.19, f32[1024]{0:T(1024)S(1)} %get-tuple-element.17, bf16[1,4,1024,4096]{3,2,1,0:T(8,128)(2,1)} %param.10, bf16[4,128,4096]{2,1,0:T(8,128)(2,1)} %all-gather.8.cloned.1.call-done, pred[4]{0:T(512)(128)(4,1)S(1)} %broadcast_compare_fusion), kind=kOutput, calls=%fused_computation.42 | convolution fusion | flops 4297718784 | bytes 38543364 | tf_op jit(solution)/shard_map/tnd,tkd->nk/dot_general | solution.py:33
  428.7 0.0 copy-done
  428.7 5.6 %convert_bitcast_fusion = bf16[1,4096,1024]{1,2,0:T(8,128)(2,1)} fusion(bf16[1,128,4096]{2,1,0:T(8,128)(2,1)S(1)} %copy-done, bf16[128,1024]{1,0:T(8,128)(2,1)S(1)} %get-tuple-element.21), kind=kOutput, calls=%fused_computation.12 | convolution fusion | flops 1077936128 | bytes 9699328 | tf_op jit(solution)/shard_map/dot_general | solution.py:38
  434.3 11.9 %copy.26 = bf16[1,4096,1024]{2,1,0:T(8,128)(2,1)} copy(bf16[1,4096,1024]{1,2,0:T(8,128)(2,1)} %convert_bitcast_fusion) | data formatting | bytes 16777216
  (4 shorter events, 0.0 us)
Async XLA Ops:
  7.2 46.0 %all-gather.10.cloned.1.call-start = ((), (), s32[]{:S(2)}) async-start(), calls=%async_computation.6 | async-start | bytes 1179648 | tf_op jit(solution)/shard_map/all_gather | solution.py:13
  7.9 139.0 %reduce-scatter.3.cloned.1.call-start = ((), (), s32[]{:S(2)}) async-start(), calls=%async_computation.2 | async-start | bytes 10485760 | tf_op jit(solution)/shard_map/reduce_scatter | solution.py:22
  76.5 142.6 %copy-start.2 = (bf16[1,16,4096]{2,1,0:T(8,128)(2,1)S(1)}, bf16[1,16,4096]{2,1,0:T(8,128)(2,1)}, u32[]{:S(2)}) copy-start(bf16[1,16,4096]{2,1,0:T(8,128)(2,1)} %param.7) | copy-start | bytes 393220
  76.5 142.6 %copy-start.3 = (f32[1,4096]{1,0:T(1,128)S(1)}, f32[1,4096]{1,0:T(1,128)}, u32[]{:S(2)}) copy-start(f32[1,4096]{1,0:T(1,128)} %param.11) | copy-start | bytes 49156
  76.6 142.6 %reduce-scatter.5.cloned.1.call-start = ((), (), s32[]{:S(2)}) async-start(), calls=%async_computation.3 | async-start | bytes 2359296 | tf_op jit(solution)/shard_map/reduce_scatter | solution.py:23
  146.9 114.2 %all-gather.6.cloned.1.call-start = ((), (), s32[]{:S(2)}) async-start(), calls=%async_computation.4 | async-start | bytes 1179648 | tf_op jit(solution)/shard_map/all_gather | solution.py:27
  220.8 124.3 %all-gather.8.cloned.1.call-start = ((), (), s32[]{:S(2)}) async-start(), calls=%async_computation.5 | async-start | bytes 5242880 | tf_op jit(solution)/shard_map/all_gather | solution.py:28
  301.6 11.9 %copy-start.1 = (f32[1,16,4096]{2,1,0:T(8,128)S(1)}, f32[1,16,4096]{2,1,0:T(8,128)}, u32[]{:S(2)}) copy-start(f32[1,16,4096]{2,1,0:T(8,128)} %reduce-scatter.5.cloned.1.call-done) | copy-start | bytes 786436
  411.1 17.6 %copy-start = (bf16[1,128,4096]{2,1,0:T(8,128)(2,1)S(1)}, bf16[1,128,4096]{2,1,0:T(8,128)(2,1)}, u32[]{:S(2)}) copy-start(bf16[1,128,4096]{2,1,0:T(8,128)(2,1)} %all-gather.10.cloned.1.call-done) | copy-start | bytes 3145732
Sparse Core Ops, SparseCore 0:
  10.1 42.9 all-gather.9
  76.7 70.1 reduce-scatter.2
  150.4 68.7 reduce-scatter.4
  221.7 39.2 all-gather.5
  262.5 33.1 all-gather.7
